TPU v7x, 32 devices: a whole 2x2x4 slice. The times are simulated.
32 devices in a mesh: batch: 4 (over x, core), seq: 8 (over z, y).
Axes of the slice: x: 2, y: 2, z: 4, core: 2. Of those that a mesh axis runs over, the one named last changes fastest.
Arguments:
- sequences: bfloat16 [4, 2048, 256], P('batch', 'seq'), may hold values from -6 to 6
- filter_taps: float32 [2048, 256], P('seq'), may hold values from -0.125 to 0.125
- w_in: bfloat16 [256, 768], replicated, may hold values from -0.375 to 0.375
- w_out: bfloat16 [256, 256], replicated, may hold values from -0.375 to 0.375
- grad_out: bfloat16 [4, 2048, 256], P('batch', 'seq'), may hold values from -6 to 6
Outputs:
- layer_out: bfloat16 [4, 2048, 256], P('batch', 'seq')
- filter_grad: float32 [2, 16, 256, 256], P(None, 'seq', 'batch')
All inputs are finite; a program needn't handle non-finite values.
Results may differ from a plain program's by a relative error of at most 0.0049.
Values sent between devices are 32-bit elements; how exact they have to be, the bound alone decides.
A program may use at most 64 MiB of HBM per device.

v0:
```python
import functools
import math

import jax
import jax.numpy as jnp
import numpy as np
from jax import lax
from jax.experimental import pallas as pl
from jax.experimental.pallas import tpu as pltpu
from jax.sharding import PartitionSpec as P

precise = lax.Precision.HIGHEST


def counting(length):
    return jnp.arange(length, dtype=jnp.int32)


def phase_table(left_index, right_index, period):
    product = left_index[:, None] * right_index[None, :] % period
    angles = product.astype(jnp.float32) * (2.0 * math.pi / period)
    return (jnp.cos(angles), jnp.sin(angles))


def split_length(length):
    outer_len = math.isqrt(length)
    while length % outer_len:
        outer_len -= 1
    return (outer_len, length // outer_len)


def local_forward(spectrum):
    groups = spectrum.shape[0]
    length = spectrum.shape[1]
    channels = spectrum.shape[3]
    outer_len, inner_len = split_length(length)
    shaped = spectrum.reshape(groups, outer_len, inner_len, 2, channels)
    real_in = shaped[:, :, :, 0]
    imag_in = shaped[:, :, :, 1]
    cos_outer, sin_outer = phase_table(counting(outer_len), counting(outer_len), outer_len)
    real_mid = jnp.einsum("jm,fmnc->fjnc", cos_outer, real_in, precision=precise) + jnp.einsum(
        "jm,fmnc->fjnc", sin_outer, imag_in, precision=precise
    )
    imag_mid = jnp.einsum("jm,fmnc->fjnc", cos_outer, imag_in, precision=precise) - jnp.einsum(
        "jm,fmnc->fjnc", sin_outer, real_in, precision=precise
    )
    cos_twist, sin_twist = phase_table(counting(outer_len), counting(inner_len), length)
    cos_twist = cos_twist[None, :, :, None]
    sin_twist = sin_twist[None, :, :, None]
    real_turned = real_mid * cos_twist + imag_mid * sin_twist
    imag_turned = imag_mid * cos_twist - real_mid * sin_twist
    cos_inner, sin_inner = phase_table(counting(inner_len), counting(inner_len), inner_len)
    real_out = jnp.einsum("kn,fjnc->fkjc", cos_inner, real_turned, precision=precise) + jnp.einsum(
        "kn,fjnc->fkjc", sin_inner, imag_turned, precision=precise
    )
    imag_out = jnp.einsum("kn,fjnc->fkjc", cos_inner, imag_turned, precision=precise) - jnp.einsum(
        "kn,fjnc->fkjc", sin_inner, real_turned, precision=precise
    )
    return jnp.stack([real_out, imag_out], axis=3).reshape(groups, length, 2, channels)


def local_inverse(real_spec, imag_spec):
    groups = real_spec.shape[0]
    length = real_spec.shape[1]
    channels = real_spec.shape[2]
    outer_len, inner_len = split_length(length)
    real_grid = real_spec.reshape(groups, inner_len, outer_len, channels)
    imag_grid = imag_spec.reshape(groups, inner_len, outer_len, channels)
    cos_inner, sin_inner = phase_table(counting(inner_len), counting(inner_len), inner_len)
    real_mid = jnp.einsum("nk,fkjc->fjnc", cos_inner, real_grid, precision=precise) - jnp.einsum(
        "nk,fkjc->fjnc", sin_inner, imag_grid, precision=precise
    )
    imag_mid = jnp.einsum("nk,fkjc->fjnc", cos_inner, imag_grid, precision=precise) + jnp.einsum(
        "nk,fkjc->fjnc", sin_inner, real_grid, precision=precise
    )
    cos_twist, sin_twist = phase_table(counting(outer_len), counting(inner_len), length)
    cos_twist = cos_twist[None, :, :, None]
    sin_twist = sin_twist[None, :, :, None]
    real_turned = real_mid * cos_twist - imag_mid * sin_twist
    imag_turned = imag_mid * cos_twist + real_mid * sin_twist
    cos_outer, sin_outer = phase_table(counting(outer_len), counting(outer_len), outer_len)
    real_out = jnp.einsum("mj,fjnc->fmnc", cos_outer, real_turned, precision=precise) - jnp.einsum(
        "mj,fjnc->fmnc", sin_outer, imag_turned, precision=precise
    )
    imag_out = jnp.einsum("mj,fjnc->fmnc", cos_outer, imag_turned, precision=precise) + jnp.einsum(
        "mj,fjnc->fmnc", sin_outer, real_turned, precision=precise
    )
    return (real_out.reshape(groups, length, channels), imag_out.reshape(groups, length, channels))


def forward_spectrum(columns, residue_order):
    shards = lax.axis_size("seq")
    local_len = columns.shape[0]
    block_rows = local_len // shards
    freq_rows = 2 * shards
    full_span = freq_rows * local_len
    glob_rows = lax.axis_index("seq") * block_rows + counting(block_rows)
    pieces = lax.all_to_all(columns[None], "seq", split_axis=1, concat_axis=0, tiled=True)
    cos_first, sin_first = phase_table(residue_order, counting(shards), freq_rows)
    real_part = jnp.einsum("ka,amc->kmc", cos_first, pieces[:, :, 0], precision=precise)
    imag_part = -jnp.einsum("ka,amc->kmc", sin_first, pieces[:, :, 0], precision=precise)
    cos_twist, sin_twist = phase_table(residue_order, glob_rows, full_span)
    cos_twist = cos_twist[:, :, None]
    sin_twist = sin_twist[:, :, None]
    real_turned = real_part * cos_twist + imag_part * sin_twist
    imag_turned = imag_part * cos_twist - real_part * sin_twist
    packed = jnp.stack([real_turned, imag_turned], axis=2)
    return local_forward(lax.all_to_all(packed, "seq", split_axis=0, concat_axis=1, tiled=True))


def inverse_signal(real_spec, imag_spec, residue_order):
    shards = lax.axis_size("seq")
    pair_rows = real_spec.shape[0]
    local_len = real_spec.shape[1]
    freq_rows = pair_rows * shards
    full_span = freq_rows * local_len
    real_part, imag_part = local_inverse(real_spec, imag_spec)
    pair_index = lax.dynamic_slice_in_dim(
        residue_order, lax.axis_index("seq") * pair_rows, pair_rows
    )
    cos_twist, sin_twist = phase_table(pair_index, counting(local_len), full_span)
    cos_twist = cos_twist[:, :, None]
    sin_twist = sin_twist[:, :, None]
    real_turned = real_part * cos_twist - imag_part * sin_twist
    imag_turned = imag_part * cos_twist + real_part * sin_twist
    packed = jnp.stack([real_turned, imag_turned], axis=2)
    pieces = lax.all_to_all(packed, "seq", split_axis=1, concat_axis=0, tiled=True)
    cos_last, sin_last = phase_table(counting(shards), residue_order, freq_rows)
    summed = jnp.einsum("ak,kmc->amc", cos_last, pieces[:, :, 0], precision=precise) - jnp.einsum(
        "ak,kmc->amc", sin_last, pieces[:, :, 1], precision=precise
    )
    columns = summed * (1.0 / full_span)
    placed = lax.all_to_all(columns, "seq", split_axis=0, concat_axis=1, tiled=True)
    return placed[0]


def local(sequences, filter_taps, w_in, w_out, grad_out):
    channels = w_out.shape[0]
    groups = lax.axis_size("batch")
    shards = lax.axis_size("seq")
    projected = jnp.dot(sequences[0], w_in, preferred_element_type=jnp.float32)
    queries = projected[:, :channels]
    signal = projected[:, channels : 2 * channels] * projected[:, 2 * channels :]
    back_grad = lax.dot_general(
        grad_out[0], w_out, (((1,), (1,)), ((), ())), preferred_element_type=jnp.float32
    )
    conv_grad = queries * back_grad
    order_table = np.arange(2 * shards)
    residue_order = jnp.asarray(order_table, jnp.int32)
    part_width = channels // groups
    filter_part = lax.dynamic_slice_in_dim(
        filter_taps, lax.axis_index("batch") * part_width, part_width, 1
    )
    signal_spec = forward_spectrum(signal[:, None], residue_order)
    grad_spec = forward_spectrum(conv_grad[:, None], residue_order)
    taps_spec = forward_spectrum(filter_part[:, None], residue_order)
    taps_spec = lax.all_gather(taps_spec, "batch", axis=3, tiled=True)
    real_sig = signal_spec[:, :, 0]
    imag_sig = signal_spec[:, :, 1]
    real_taps = taps_spec[:, :, 0]
    imag_taps = taps_spec[:, :, 1]
    real_conv = real_taps * real_sig - imag_taps * imag_sig
    imag_conv = real_taps * imag_sig + imag_taps * real_sig
    convolved = inverse_signal(real_conv, imag_conv, residue_order)
    gated = (queries * convolved).astype(jnp.bfloat16)
    layer_out = jnp.dot(gated, w_out, preferred_element_type=jnp.float32).astype(jnp.bfloat16)
    factor = 1.0 / (signal_spec.shape[0] * shards * signal_spec.shape[1])
    real_grad = grad_spec[:, :, 0]
    imag_grad = grad_spec[:, :, 1]
    grad_terms = jnp.stack(
        [
            (real_sig * real_grad + imag_sig * imag_grad) * factor,
            (real_sig * imag_grad - imag_sig * real_grad) * factor,
        ],
        axis=0,
    )
    filter_grad = lax.psum_scatter(grad_terms, "batch", scatter_dimension=2, tiled=True)
    return (layer_out[None], filter_grad)


MESH = pl.DeviceIdType.MESH
FULL_TILE = 8


def wide_tables(block_rows, freq_rows):
    residues = freq_rows // 2 + 1
    span = block_rows * freq_rows
    near = np.arange(block_rows)
    angles = 2.0 * np.pi * (np.outer(near, near) % block_rows) / block_rows
    cos_part, sin_part = np.cos(angles), np.sin(angles)
    matrix = np.block([[cos_part, -sin_part], [sin_part, cos_part]])
    high = matrix.astype(jnp.bfloat16)
    low = (matrix - high.astype(np.float64)).astype(jnp.bfloat16)
    twist_angles = 2.0 * np.pi * np.outer(np.arange(residues), near) / span
    twist = np.stack([np.cos(twist_angles), np.sin(twist_angles)], axis=0).astype(np.float32)
    twist = np.ascontiguousarray(
        np.broadcast_to(twist[:, :, None, :], (2, residues, FULL_TILE, block_rows))
    )
    return (high, low, twist)


def grouped_sum(items, weights):
    groups = {}
    for item, weight in zip(items, weights):
        size = round(abs(weight), 12)
        if size == 0.0:
            continue
        positive, total = groups.get(size, (None, None))
        if total is None:
            groups[size] = (weight > 0, item)
        elif positive == (weight > 0):
            groups[size] = (positive, total + item)
        else:
            groups[size] = (positive, total - item)
    result = None
    for size in sorted(groups, reverse=True):
        positive, total = groups[size]
        term = total if size == 1.0 else total * size
        if result is None:
            result = term if positive else -term
        else:
            result = result + term if positive else result - term
    return result


def kernel(
    groups, shards, part,
    x_hbm, taps_hbm, w_in_hbm, w_out_hbm, cot_hbm, high_hbm, low_hbm, twist_hbm,
    out_hbm, spec_out,
    x_ref, taps_ref, w_in_ref, w_out_ref, cot_ref, high_ref, low_ref, twist_ref, out_ref,
    load_sems, store_sems, query_buf, sig_send, cot_send, tap_send, sig_buf, cot_buf, tap_buf,
    conv_send, conv_buf, spec_send,
    work, sig_spec, tap_spec, send_sems, recv_sems,
):
    count = groups * shards
    rows = x_ref.shape[1]
    channels = w_out_ref.shape[0]
    freq_rows = 2 * shards
    residues = shards + 1
    lanes = rows // groups
    my_group = lax.axis_index("batch")
    my_shard = lax.axis_index("seq")
    me = my_group * shards + my_shard
    barrier = pltpu.get_barrier_semaphore()

    half = shards // 2
    my_half = lax.div(my_shard, half)

    def place(step):
        side = 1 - lax.div(step, half * groups)
        inner = lax.rem(step, half * groups) + (1 - side)
        group = lax.rem(my_group + inner, groups)
        turn = lax.div(inner, groups)
        if half % 2 == 0:
            distant = turn + lax.rem(my_shard, 2) * (1 - 2 * lax.rem(turn, 2))
        else:
            distant = turn
        distant = (1 - my_half) * (shards - 1 - distant) + my_half * distant
        close = my_half * half + lax.rem(my_shard + turn, half)
        shard = side * distant + (1 - side) * close
        return (group * shards + shard, group, shard)

    def greet(step, carry):
        _, group, shard = place(step)
        pl.semaphore_signal(barrier, inc=1, device_id=(group, shard), device_id_type=MESH)
        return carry

    lax.fori_loop(0, count - 1, greet, 0, unroll=True)
    loads = [
        pltpu.make_async_copy(source, target, load_sems.at[n])
        for n, (source, target) in enumerate(
            (
                (x_hbm, x_ref),
                (w_in_hbm, w_in_ref),
                (taps_hbm, taps_ref),
                (w_out_hbm, w_out_ref),
                (cot_hbm, cot_ref),
                (twist_hbm, twist_ref),
                (high_hbm, high_ref),
                (low_hbm, low_ref),
            )
        )
    ]
    for load in loads:
        load.start()
    loads[0].wait()
    loads[1].wait()

    def send_all(source, target, slot, keep=True):
        def one(step, carry):
            other, group, shard = place(step)
            pltpu.make_async_remote_copy(
                src_ref=source.at[other],
                dst_ref=target.at[me],
                send_sem=send_sems.at[slot],
                recv_sem=recv_sems.at[slot],
                device_id=(group, shard),
                device_id_type=MESH,
            ).start()
            return carry

        lax.fori_loop(0, count - 1, one, 0, unroll=True)
        if keep:
            target[me] = source[me]

    def bundle(source, target, slot, many):
        return pltpu.make_async_remote_copy(
            src_ref=source.at[pl.ds(0, many)],
            dst_ref=target.at[pl.ds(0, many)],
            send_sem=send_sems.at[slot],
            recv_sem=recv_sems.at[slot],
            device_id=(my_group, my_shard),
            device_id_type=MESH,
        )

    projected = lax.dot_general(
        w_in_ref[...], x_ref[0], (((0,), (1,)), ((), ())), preferred_element_type=jnp.float32
    )
    queries = projected[:channels]
    query_buf[...] = queries
    signal = projected[channels : 2 * channels] * projected[2 * channels :]
    sig_send[...] = signal.reshape(count, part, rows)
    loads[2].wait()
    tap_send[...] = taps_ref[...].T.reshape(count, part, rows)
    pl.semaphore_wait(barrier, count - 1)
    send_all(sig_send, sig_buf, 0)

    def send_taps(step, carry):
        shard = lax.rem(my_shard + step, shards)
        pltpu.make_async_remote_copy(
            src_ref=tap_send.at[my_group * shards + shard],
            dst_ref=tap_buf.at[my_shard],
            send_sem=send_sems.at[1],
            recv_sem=recv_sems.at[1],
            device_id=(my_group, shard),
            device_id_type=MESH,
        ).start()
        return carry

    lax.fori_loop(1, shards, send_taps, 0)
    tap_buf[my_shard] = tap_send[me]
    loads[3].wait()
    loads[4].wait()
    back = lax.dot_general(
        w_out_ref[...], cot_ref[0], (((1,), (1,)), ((), ())), preferred_element_type=jnp.float32
    )
    cot_send[...] = (queries * back).reshape(count, part, rows)
    send_all(cot_send, cot_buf, 2)

    def multiply(value):
        top = value.astype(jnp.bfloat16)
        rest = (value - top.astype(jnp.float32)).astype(jnp.bfloat16)
        high = high_ref[...]
        return (
            jnp.dot(top, high, preferred_element_type=jnp.float32)
            + jnp.dot(rest, high, preferred_element_type=jnp.float32)
            + jnp.dot(top, low_ref[...], preferred_element_type=jnp.float32)
        )

    for load in loads[5:]:
        load.wait()
    turns = 2.0 * math.pi / freq_rows

    def forward(blocks, height):
        for index in range(residues):
            real_part = grouped_sum(
                blocks, [math.cos(turns * (a * index % freq_rows)) for a in range(shards)]
            )
            imag_part = grouped_sum(
                blocks, [-math.sin(turns * (a * index % freq_rows)) for a in range(shards)]
            )
            cos_t = twist_ref[0, index][None]
            sin_t = twist_ref[1, index][None]
            if imag_part is None:
                real_turned = real_part * cos_t
                imag_turned = -(real_part * sin_t)
            else:
                real_turned = real_part * cos_t + imag_part * sin_t
                imag_turned = imag_part * cos_t - real_part * sin_t
            place_at = pl.ds(index * height, height)
            work[place_at, :rows] = real_turned.reshape(height, rows)
            work[place_at, rows:] = imag_turned.reshape(height, rows)
        return multiply(work[pl.ds(0, residues * height), :])

    height = groups * part
    bundle(sig_send, sig_buf, 0, count - 1).wait_recv()
    by_source = sig_buf[...].reshape(groups, shards, part, rows)
    sig_spec[...] = forward([by_source[:, a] for a in range(shards)], height)

    bundle(tap_send, tap_buf, 1, shards - 1).wait_recv()
    tap_blocks = tap_buf[...]
    tap_spec[...] = forward([tap_blocks[a][None] for a in range(shards)], part)

    factor = 1.0 / (freq_rows * rows)
    for index in range(residues):
        weight = factor if index in (0, shards) else 2.0 * factor
        tap_part = tap_spec[pl.ds(index * part, part), :] * weight
        real_tap = tap_part[None, :, :rows]
        imag_tap = tap_part[None, :, rows:]
        sig_part = sig_spec[pl.ds(index * height, height), :].reshape(groups, part, 2 * rows)
        real_sig = sig_part[:, :, :rows]
        imag_sig = sig_part[:, :, rows:]
        place_at = pl.ds(index * height, height)
        work[place_at, :rows] = (real_tap * real_sig - imag_tap * imag_sig).reshape(height, rows)
        work[place_at, rows:] = -(real_tap * imag_sig + imag_tap * real_sig).reshape(height, rows)
    work[...] = multiply(work[...])
    real_items = []
    imag_items = []
    for index in range(residues):
        piece = work[pl.ds(index * height, height), :].reshape(groups, part, 2 * rows)
        cos_t = twist_ref[0, index][None]
        sin_t = twist_ref[1, index][None]
        real_items.append(piece[:, :, :rows] * cos_t + piece[:, :, rows:] * sin_t)
        imag_items.append(piece[:, :, :rows] * sin_t - piece[:, :, rows:] * cos_t)
    for a in range(shards):
        value = grouped_sum(
            real_items + imag_items,
            [math.cos(turns * (a * i % freq_rows)) for i in range(residues)]
            + [-math.sin(turns * (a * i % freq_rows)) for i in range(residues)],
        )
        for group in range(groups):
            conv_send[group * shards + a] = value[group]
    send_all(conv_send, conv_buf, 3)

    bundle(cot_send, cot_buf, 2, count - 1).wait_recv()
    by_source = cot_buf[...].reshape(groups, shards, part, rows)
    work[...] = forward([by_source[:, a] for a in range(shards)], height)
    real_spec = []
    imag_spec = []
    for index in range(residues):
        place_at = pl.ds(index * height, height)
        sig_part = (sig_spec[place_at, :] * factor).reshape(groups, part, 2 * rows)
        cot_part = work[place_at, :].reshape(groups, part, 2 * rows)
        real_sig, imag_sig = sig_part[:, :, :rows], sig_part[:, :, rows:]
        real_cot, imag_cot = cot_part[:, :, :rows], cot_part[:, :, rows:]
        real_spec.append(jnp.sum(real_sig * real_cot + imag_sig * imag_cot, axis=0))
        imag_spec.append(jnp.sum(real_sig * imag_cot - imag_sig * real_cot, axis=0))
    row = lax.broadcasted_iota(jnp.int32, (rows, rows), 0)
    column = lax.broadcasted_iota(jnp.int32, (rows, rows), 1)
    reverse = jnp.where(row + column == rows - 1, 1.0, 0.0).astype(jnp.bfloat16)
    straight = jnp.concatenate(
        real_spec[1:shards] + [-piece for piece in imag_spec[1:shards]], axis=0
    )
    turned = None
    for _ in range(3):
        top = straight.astype(jnp.bfloat16)
        straight = straight - top.astype(jnp.float32)
        term = jnp.dot(top, reverse, preferred_element_type=jnp.float32)
        turned = term if turned is None else turned + term
    for index in range(shards - 1, 0, -1):
        low_row = (index - 1) * part
        real_spec.append(turned[low_row : low_row + part])
        low_row += (shards - 1) * part
        imag_spec.append(turned[low_row : low_row + part])
    for shard in range(shards):
        for group in range(groups):
            pieces = [
                spec[index][:, group * lanes : (group + 1) * lanes]
                for spec in (real_spec, imag_spec)
                for index in (2 * shard, 2 * shard + 1)
            ]
            spec_send[group * shards + shard] = jnp.concatenate(pieces, axis=1)
    send_all(spec_send, spec_out, 4, keep=False)
    own = pltpu.make_async_copy(spec_send.at[me], spec_out.at[me], store_sems.at[0])
    own.start()

    bundle(conv_send, conv_buf, 3, count - 1).wait_recv()
    gated = (query_buf[...] * conv_buf[...].reshape(channels, rows)).astype(jnp.bfloat16)
    out_ref[0] = lax.dot_general(
        gated, w_out_ref[...], (((0,), (0,)), ((), ())), preferred_element_type=jnp.float32
    ).astype(jnp.bfloat16)

    store = pltpu.make_async_copy(out_ref, out_hbm, store_sems.at[1])
    store.start()
    bundle(sig_send, sig_buf, 0, count - 1).wait_send()
    bundle(tap_send, tap_buf, 1, shards - 1).wait_send()
    bundle(cot_send, cot_buf, 2, count - 1).wait_send()
    bundle(conv_send, conv_buf, 3, count - 1).wait_send()
    bundle(spec_send, spec_out, 4, count - 1).wait_send()
    own.wait()
    store.wait()
    bundle(spec_send, spec_out, 4, count - 1).wait_recv()


def finish(raw_hbm, spec_hbm, out_hbm, grad_hbm, raw_buf, spec_buf, grad_buf, load_sems, store_sems):
    load_spec = pltpu.make_async_copy(spec_hbm, spec_buf, load_sems.at[0])
    load_raw = pltpu.make_async_copy(raw_hbm, raw_buf, load_sems.at[1])
    load_spec.start()
    load_raw.start()
    count, part, width = spec_buf.shape
    stores = []
    load_spec.wait()
    for kind in range(2):
        piece = spec_buf[:, :, kind * (width // 2) : (kind + 1) * (width // 2)]
        grad_buf[kind] = piece.reshape(count * part, width // 2).T.reshape(grad_buf.shape[1:])
        store = pltpu.make_async_copy(grad_buf.at[kind], grad_hbm.at[kind], store_sems.at[kind])
        store.start()
        stores.append(store)
        if kind == 0:
            load_raw.wait()
            store = pltpu.make_async_copy(raw_buf, out_hbm, store_sems.at[2])
            store.start()
            stores.append(store)
    for store in stores:
        store.wait()


def direct(sequences, filter_taps, w_in, w_out, grad_out):
    groups = lax.axis_size("batch")
    shards = lax.axis_size("seq")
    rows = sequences.shape[1]
    channels = w_out.shape[0]
    count = groups * shards
    part = channels // count
    freq_rows = 2 * shards
    residues = shards + 1
    lanes = rows // groups
    high, low, twist = wide_tables(rows, freq_rows)
    operands = (
        sequences, filter_taps, w_in, w_out, grad_out,
        jnp.asarray(high), jnp.asarray(low), jnp.asarray(twist),
    )
    chunk = pltpu.VMEM((count, part, rows), jnp.float32)
    height = groups * part
    anywhere = pl.BlockSpec(memory_space=pl.ANY)
    raw, spectra = pl.pallas_call(
        functools.partial(kernel, groups, shards, part),
        out_shape=(
            jax.ShapeDtypeStruct((1, rows, channels), jnp.bfloat16),
            jax.ShapeDtypeStruct((count, part, rows), jnp.float32),
        ),
        in_specs=[anywhere] * 8,
        out_specs=(anywhere, anywhere),
        scratch_shapes=[
            *(pltpu.VMEM(item.shape, item.dtype) for item in operands),
            pltpu.VMEM((1, rows, channels), jnp.bfloat16),
            pltpu.SemaphoreType.DMA((8,)),
            pltpu.SemaphoreType.DMA((2,)),
            pltpu.VMEM((channels, rows), jnp.float32),
            chunk,
            chunk,
            chunk,
            chunk,
            chunk,
            pltpu.VMEM((shards, part, rows), jnp.float32),
            chunk,
            chunk,
            chunk,
            pltpu.VMEM((residues * height, 2 * rows), jnp.float32),
            pltpu.VMEM((residues * height, 2 * rows), jnp.float32),
            pltpu.VMEM((residues * part, 2 * rows), jnp.float32),
            pltpu.SemaphoreType.DMA((5,)),
            pltpu.SemaphoreType.DMA((5,)),
        ],
        compiler_params=pltpu.CompilerParams(collective_id=0, has_side_effects=True),
    )(*operands)
    return pl.pallas_call(
        finish,
        out_shape=(
            jax.ShapeDtypeStruct((1, rows, channels), jnp.bfloat16),
            jax.ShapeDtypeStruct((2, 2, lanes, channels), jnp.float32),
        ),
        in_specs=[anywhere] * 2,
        out_specs=(anywhere, anywhere),
        scratch_shapes=[
            pltpu.VMEM(raw.shape, raw.dtype),
            pltpu.VMEM(spectra.shape, spectra.dtype),
            pltpu.VMEM((2, 2, lanes, channels), jnp.float32),
            pltpu.SemaphoreType.DMA((2,)),
            pltpu.SemaphoreType.DMA((3,)),
        ],
    )(raw, spectra)


def body(sequences, filter_taps, w_in, w_out, grad_out):
    groups = lax.axis_size("batch")
    count = groups * lax.axis_size("seq")
    rows = sequences.shape[1]
    fits = (
        sequences.shape[0] == 1
        and w_out.shape[0] == FULL_TILE * count
        and lax.axis_size("seq") % 2 == 0
        and rows % 128 == 0
        and rows % groups == 0
        and 2 * (rows // groups) % 128 == 0
    )
    chosen = direct if fits else local
    return chosen(sequences, filter_taps, w_in, w_out, grad_out)


def solution(mesh):
    placed = (P("batch", "seq", None), P("seq", None), P(), P(), P("batch", "seq", None))
    return jax.shard_map(
        body,
        mesh=mesh,
        in_specs=placed,
        out_specs=(P("batch", "seq", None), P(None, "seq", "batch", None)),
        check_vma=False,
    )
```

profile of v0, /device:TPU:0, one launch (start us, length us, event | category | flops | bytes accessed | tf_op | source)
XLA Modules:
  0.0 35.8 jit_solution(8305043359426014283)
XLA Ops:
  0.6 33.3 %shard_map.95 = (bf16[1,256,256]{2,1,0:T(8,128)(2,1)}, f32[32,8,256]{2,1,0:T(8,128)}) custom-call(bf16[1,256,256]{2,1,0:T(8,128)(2,1)} %x_hbm.1, f32[256,256]{1,0:T(8,128)} %taps_hbm.1, bf16[256,768]{1,0:T(8,128)(2,1)} %w_in_hbm.1, bf16[256,256]{1,0:T(8,128)(2,1)} %w_out_hbm.1, bf16[1,256,256]{2,1,0:T(8,128)(2,1)} %cot_hbm.1, ...), custom_call_target="tpu_custom_call" | custom-call | tf_op jit(solution)/shard_map/pallas_call | solution.py:526
  34.0 1.9 %shard_map.96 = (bf16[1,256,256]{2,1,0:T(8,128)(2,1)}, f32[2,2,64,256]{3,2,1,0:T(8,128)}) custom-call(bf16[1,256,256]{2,1,0:T(8,128)(2,1)} %get-tuple-element.4.raw_hbm, f32[32,8,256]{2,1,0:T(8,128)} %get-tuple-element.5.spec_hbm), custom_call_target="tpu_custom_call" | custom-call | tf_op jit(solution)/shard_map/pallas_call | solution.py:557
where the time goes:
time: 36 us; the launch traced here: 35.8 us
  Pallas kernels  35.2 us (98%)
  between operations  0.64 us (2%)
    pallas_call x1, Pallas kernels, direct(): pl.pallas_call(functools.partial(kernel, groups, shards, part), out_shape...  33.3 us
    pallas_call x1, Pallas kernels, direct(): pl.pallas_call(finish, out_shape=(jax.ShapeDtypeStruct((1, rows, channels...  1.85 us

commit v1 on v0

--- a/solution.py
+++ b/solution.py
@@ -229,43 +229,60 @@
     out_hbm, spec_out,
     x_ref, taps_ref, w_in_ref, w_out_ref, cot_ref, high_ref, low_ref, twist_ref, out_ref,
     load_sems, store_sems, query_buf, sig_send, cot_send, tap_send, sig_buf, cot_buf, tap_buf,
-    conv_send, conv_buf, spec_send,
-    work, sig_spec, tap_spec, send_sems, recv_sems,
+    conv_send, conv_buf, spec_send, near_sig, near_tap, near_conv,
+    work, sig_spec, tap_spec, send_sems, recv_sems, late,
 ):
     count = groups * shards
     rows = x_ref.shape[1]
     channels = w_out_ref.shape[0]
-    freq_rows = 2 * shards
-    residues = shards + 1
+    half = shards // 2
+    quarter = shards // 4
     lanes = rows // groups
     my_group = lax.axis_index("batch")
     my_shard = lax.axis_index("seq")
     me = my_group * shards + my_shard
+    my_half = lax.div(my_shard, half)
+    lower = my_half == 0
+    upper = my_half == 1
+    is_last = my_shard >= shards - quarter
+    near_me = my_group * half + lax.rem(my_shard, half)
     barrier = pltpu.get_barrier_semaphore()
 
-    half = shards // 2
-    my_half = lax.div(my_shard, half)
-
-    def place(step):
-        side = 1 - lax.div(step, half * groups)
-        inner = lax.rem(step, half * groups) + (1 - side)
-        group = lax.rem(my_group + inner, groups)
-        turn = lax.div(inner, groups)
-        if half % 2 == 0:
-            distant = turn + lax.rem(my_shard, 2) * (1 - 2 * lax.rem(turn, 2))
-        else:
-            distant = turn
-        distant = (1 - my_half) * (shards - 1 - distant) + my_half * distant
-        close = my_half * half + lax.rem(my_shard + turn, half)
-        shard = side * distant + (1 - side) * close
-        return (group * shards + shard, group, shard)
-
-    def greet(step, carry):
-        _, group, shard = place(step)
-        pl.semaphore_signal(barrier, inc=1, device_id=(group, shard), device_id_type=MESH)
-        return carry
-
-    lax.fori_loop(0, count - 1, greet, 0, unroll=True)
+    def across(step):
+        turn = step // groups
+        shard = (1 - my_half) * half + turn // quarter * quarter + lax.rem(my_shard + turn, quarter)
+        return (lax.rem(my_group + step, groups), shard)
+
+    def level(step):
+        turn = step // groups
+        shard = lax.div(my_shard, quarter) * quarter + lax.rem(my_shard + turn, quarter)
+        return (lax.rem(my_group + step, groups), shard)
+
+    def beside(step):
+        turn = step // groups
+        plane = 2 * my_half + 1 - lax.rem(lax.div(my_shard, quarter), 2)
+        return (lax.rem(my_group + step, groups), plane * quarter + lax.rem(my_shard + turn, quarter))
+
+    wide = groups * quarter
+    far_first = [across(step) for step in range(wide)]
+    far_second = [across(step) for step in range(wide, 2 * wide)]
+    far = far_first + far_second
+    same_plane = [level(step) for step in range(1, wide)]
+    next_plane = [beside(step) for step in range(wide)]
+    near = next_plane + same_plane
+
+    def signal(semaphore, peers):
+        for group, shard in peers:
+            pl.semaphore_signal(semaphore, inc=1, device_id=(group, shard), device_id_type=MESH)
+
+    @pl.when(jnp.logical_not(is_last))
+    def _():
+        signal(barrier, far + near)
+
+    @pl.when(is_last)
+    def _():
+        signal(barrier, same_plane)
+
     loads = [
         pltpu.make_async_copy(source, target, load_sems.at[n])
         for n, (source, target) in enumerate(
@@ -283,25 +300,29 @@
     ]
     for load in loads:
         load.start()
-    loads[0].wait()
-    loads[1].wait()
-
-    def send_all(source, target, slot, keep=True):
-        def one(step, carry):
-            other, group, shard = place(step)
+
+    def push(source, target, slot, peers):
+        for group, shard in peers:
             pltpu.make_async_remote_copy(
-                src_ref=source.at[other],
+                src_ref=source.at[group * shards + shard],
                 dst_ref=target.at[me],
                 send_sem=send_sems.at[slot],
                 recv_sem=recv_sems.at[slot],
                 device_id=(group, shard),
                 device_id_type=MESH,
             ).start()
-            return carry
-
-        lax.fori_loop(0, count - 1, one, 0, unroll=True)
-        if keep:
-            target[me] = source[me]
+
+    def push_taps(offsets):
+        for offset in offsets:
+            shard = lax.rem(my_shard + offset, shards)
+            pltpu.make_async_remote_copy(
+                src_ref=tap_send.at[my_group * shards + shard],
+                dst_ref=tap_buf.at[my_shard],
+                send_sem=send_sems.at[1],
+                recv_sem=recv_sems.at[1],
+                device_id=(my_group, shard),
+                device_id_type=MESH,
+            ).start()
 
     def bundle(source, target, slot, many):
         return pltpu.make_async_remote_copy(
@@ -313,31 +334,53 @@
             device_id_type=MESH,
         )
 
+    loads[0].wait()
+    loads[1].wait()
     projected = lax.dot_general(
         w_in_ref[...], x_ref[0], (((0,), (1,)), ((), ())), preferred_element_type=jnp.float32
     )
     queries = projected[:channels]
     query_buf[...] = queries
-    signal = projected[channels : 2 * channels] * projected[2 * channels :]
-    sig_send[...] = signal.reshape(count, part, rows)
+    signal_part = projected[channels : 2 * channels] * projected[2 * channels :]
+    sig_send[...] = signal_part.reshape(count, part, rows)
     loads[2].wait()
     tap_send[...] = taps_ref[...].T.reshape(count, part, rows)
-    pl.semaphore_wait(barrier, count - 1)
-    send_all(sig_send, sig_buf, 0)
-
-    def send_taps(step, carry):
-        shard = lax.rem(my_shard + step, shards)
-        pltpu.make_async_remote_copy(
-            src_ref=tap_send.at[my_group * shards + shard],
-            dst_ref=tap_buf.at[my_shard],
-            send_sem=send_sems.at[1],
-            recv_sem=recv_sems.at[1],
-            device_id=(my_group, shard),
-            device_id_type=MESH,
-        ).start()
-        return carry
-
-    lax.fori_loop(1, shards, send_taps, 0)
+    pl.semaphore_wait(barrier, jnp.where(is_last, count - 1, count - 1 - wide))
+
+    @pl.when(is_last)
+    def _():
+        signal(late, far + next_plane)
+
+    @pl.when(lower)
+    def _():
+        push(sig_send, sig_buf, 0, far_first + near)
+        for group, shard in near:
+            pltpu.make_async_remote_copy(
+                src_ref=sig_send.at[group * shards + shard + half],
+                dst_ref=near_sig.at[near_me],
+                send_sem=send_sems.at[5],
+                recv_sem=recv_sems.at[5],
+                device_id=(group, shard),
+                device_id_type=MESH,
+            ).start()
+        near_sig[near_me] = sig_send[me + half]
+        for offset in range(1, half):
+            shard = lax.rem(my_shard + offset, half)
+            pltpu.make_async_remote_copy(
+                src_ref=tap_send.at[my_group * shards + shard + half],
+                dst_ref=near_tap.at[my_shard],
+                send_sem=send_sems.at[6],
+                recv_sem=recv_sems.at[6],
+                device_id=(my_group, shard),
+                device_id_type=MESH,
+            ).start()
+        near_tap[my_shard] = tap_send[me + half]
+
+    @pl.when(upper)
+    def _():
+        push(sig_send, sig_buf, 0, far + same_plane)
+
+    sig_buf[me] = sig_send[me]
     tap_buf[my_shard] = tap_send[me]
     loads[3].wait()
     loads[4].wait()
@@ -345,7 +388,23 @@
         w_out_ref[...], cot_ref[0], (((1,), (1,)), ((), ())), preferred_element_type=jnp.float32
     )
     cot_send[...] = (queries * back).reshape(count, part, rows)
-    send_all(cot_send, cot_buf, 2)
+
+    @pl.when(jnp.logical_not(is_last))
+    def _():
+        pl.semaphore_wait(late, wide)
+
+    @pl.when(lower)
+    def _():
+        push(sig_send, sig_buf, 0, far_second)
+
+    @pl.when(upper)
+    def _():
+        push(sig_send, sig_buf, 0, next_plane)
+
+    push(cot_send, cot_buf, 2, far)
+    push_taps(range(1, shards))
+    push(cot_send, cot_buf, 2, near)
+    cot_buf[me] = cot_send[me]
 
     def multiply(value):
         top = value.astype(jnp.bfloat16)
@@ -359,18 +418,19 @@
 
     for load in loads[5:]:
         load.wait()
-    turns = 2.0 * math.pi / freq_rows
 
     def forward(blocks, height):
-        for index in range(residues):
+        bands = len(blocks)
+        turns = math.pi / bands
+        for index in range(bands + 1):
             real_part = grouped_sum(
-                blocks, [math.cos(turns * (a * index % freq_rows)) for a in range(shards)]
+                blocks, [math.cos(turns * (a * index % (2 * bands))) for a in range(bands)]
             )
             imag_part = grouped_sum(
-                blocks, [-math.sin(turns * (a * index % freq_rows)) for a in range(shards)]
+                blocks, [-math.sin(turns * (a * index % (2 * bands))) for a in range(bands)]
             )
-            cos_t = twist_ref[0, index][None]
-            sin_t = twist_ref[1, index][None]
+            cos_t = twist_ref[0, index * (shards // bands)][None]
+            sin_t = twist_ref[1, index * (shards // bands)][None]
             if imag_part is None:
                 real_turned = real_part * cos_t
                 imag_turned = -(real_part * sin_t)
@@ -380,9 +440,67 @@
             place_at = pl.ds(index * height, height)
             work[place_at, :rows] = real_turned.reshape(height, rows)
             work[place_at, rows:] = imag_turned.reshape(height, rows)
-        return multiply(work[pl.ds(0, residues * height), :])
+        return multiply(work[pl.ds(0, (bands + 1) * height), :])
 
     height = groups * part
+
+    def convolve(bands, target, stride):
+        turns = math.pi / bands
+        scale = 1.0 / (2 * bands * rows)
+        used = pl.ds(0, (bands + 1) * height)
+        for index in range(bands + 1):
+            weight = scale if index in (0, bands) else 2.0 * scale
+            tap_part = tap_spec[pl.ds(index * part, part), :] * weight
+            real_tap = tap_part[None, :, :rows]
+            imag_tap = tap_part[None, :, rows:]
+            sig_part = sig_spec[pl.ds(index * height, height), :].reshape(groups, part, 2 * rows)
+            real_sig = sig_part[:, :, :rows]
+            imag_sig = sig_part[:, :, rows:]
+            place_at = pl.ds(index * height, height)
+            work[place_at, :rows] = (real_tap * real_sig - imag_tap * imag_sig).reshape(height, rows)
+            work[place_at, rows:] = -(real_tap * imag_sig + imag_tap * real_sig).reshape(height, rows)
+        work[used, :] = multiply(work[used, :])
+        real_items = []
+        imag_items = []
+        for index in range(bands + 1):
+            piece = work[pl.ds(index * height, height), :].reshape(groups, part, 2 * rows)
+            cos_t = twist_ref[0, index * (shards // bands)][None]
+            sin_t = twist_ref[1, index * (shards // bands)][None]
+            real_items.append(piece[:, :, :rows] * cos_t + piece[:, :, rows:] * sin_t)
+            imag_items.append(piece[:, :, :rows] * sin_t - piece[:, :, rows:] * cos_t)
+        for a in range(bands):
+            value = grouped_sum(
+                real_items + imag_items,
+                [math.cos(turns * (a * i % (2 * bands))) for i in range(bands + 1)]
+                + [-math.sin(turns * (a * i % (2 * bands))) for i in range(bands + 1)],
+            )
+            for group in range(groups):
+                target[group * stride + a] = value[group]
+
+    @pl.when(lower)
+    def _():
+        bundle(sig_send, near_sig, 5, groups * half - 1).wait_recv()
+        by_source = near_sig[...].reshape(groups, half, part, rows)
+        sig_spec[pl.ds(0, (half + 1) * height), :] = forward(
+            [by_source[:, a] for a in range(half)], height
+        )
+        bundle(tap_send, near_tap, 6, half - 1).wait_recv()
+        tap_blocks = near_tap[...]
+        tap_spec[pl.ds(0, (half + 1) * part), :] = forward(
+            [tap_blocks[a][None] for a in range(half)], part
+        )
+        convolve(half, near_conv, half)
+        for group, shard in near:
+            pltpu.make_async_remote_copy(
+                src_ref=near_conv.at[group * half + shard],
+                dst_ref=conv_buf.at[me + half],
+                send_sem=send_sems.at[7],
+                recv_sem=recv_sems.at[3],
+                device_id=(group, shard),
+                device_id_type=MESH,
+            ).start()
+        conv_buf[me + half] = near_conv[near_me]
+
     bundle(sig_send, sig_buf, 0, count - 1).wait_recv()
     by_source = sig_buf[...].reshape(groups, shards, part, rows)
     sig_spec[...] = forward([by_source[:, a] for a in range(shards)], height)
@@ -390,38 +508,17 @@
     bundle(tap_send, tap_buf, 1, shards - 1).wait_recv()
     tap_blocks = tap_buf[...]
     tap_spec[...] = forward([tap_blocks[a][None] for a in range(shards)], part)
-
-    factor = 1.0 / (freq_rows * rows)
-    for index in range(residues):
-        weight = factor if index in (0, shards) else 2.0 * factor
-        tap_part = tap_spec[pl.ds(index * part, part), :] * weight
-        real_tap = tap_part[None, :, :rows]
-        imag_tap = tap_part[None, :, rows:]
-        sig_part = sig_spec[pl.ds(index * height, height), :].reshape(groups, part, 2 * rows)
-        real_sig = sig_part[:, :, :rows]
-        imag_sig = sig_part[:, :, rows:]
-        place_at = pl.ds(index * height, height)
-        work[place_at, :rows] = (real_tap * real_sig - imag_tap * imag_sig).reshape(height, rows)
-        work[place_at, rows:] = -(real_tap * imag_sig + imag_tap * real_sig).reshape(height, rows)
-    work[...] = multiply(work[...])
-    real_items = []
-    imag_items = []
-    for index in range(residues):
-        piece = work[pl.ds(index * height, height), :].reshape(groups, part, 2 * rows)
-        cos_t = twist_ref[0, index][None]
-        sin_t = twist_ref[1, index][None]
-        real_items.append(piece[:, :, :rows] * cos_t + piece[:, :, rows:] * sin_t)
-        imag_items.append(piece[:, :, :rows] * sin_t - piece[:, :, rows:] * cos_t)
-    for a in range(shards):
-        value = grouped_sum(
-            real_items + imag_items,
-            [math.cos(turns * (a * i % freq_rows)) for i in range(residues)]
-            + [-math.sin(turns * (a * i % freq_rows)) for i in range(residues)],
-        )
-        for group in range(groups):
-            conv_send[group * shards + a] = value[group]
-    send_all(conv_send, conv_buf, 3)
-
+    convolve(shards, conv_send, shards)
+
+    @pl.when(lower)
+    def _():
+        push(conv_send, conv_buf, 3, far)
+
+    push(conv_send, conv_buf, 3, near)
+    conv_buf[me] = conv_send[me]
+
+    factor = 1.0 / (2 * shards * rows)
+    residues = shards + 1
     bundle(cot_send, cot_buf, 2, count - 1).wait_recv()
     by_source = cot_buf[...].reshape(groups, shards, part, rows)
     work[...] = forward([by_source[:, a] for a in range(shards)], height)
@@ -460,11 +557,18 @@
                 for index in (2 * shard, 2 * shard + 1)
             ]
             spec_send[group * shards + shard] = jnp.concatenate(pieces, axis=1)
-    send_all(spec_send, spec_out, 4, keep=False)
+    push(spec_send, spec_out, 4, far + near)
     own = pltpu.make_async_copy(spec_send.at[me], spec_out.at[me], store_sems.at[0])
     own.start()
 
-    bundle(conv_send, conv_buf, 3, count - 1).wait_recv()
+    @pl.when(lower)
+    def _():
+        bundle(conv_send, conv_buf, 3, count - 2).wait_recv()
+
+    @pl.when(upper)
+    def _():
+        bundle(conv_send, conv_buf, 3, count - 1).wait_recv()
+
     gated = (query_buf[...] * conv_buf[...].reshape(channels, rows)).astype(jnp.bfloat16)
     out_ref[0] = lax.dot_general(
         gated, w_out_ref[...], (((0,), (0,)), ((), ())), preferred_element_type=jnp.float32
@@ -475,7 +579,18 @@
     bundle(sig_send, sig_buf, 0, count - 1).wait_send()
     bundle(tap_send, tap_buf, 1, shards - 1).wait_send()
     bundle(cot_send, cot_buf, 2, count - 1).wait_send()
-    bundle(conv_send, conv_buf, 3, count - 1).wait_send()
+
+    @pl.when(lower)
+    def _():
+        bundle(conv_send, conv_buf, 3, count - 1).wait_send()
+        bundle(sig_send, near_sig, 5, groups * half - 1).wait_send()
+        bundle(tap_send, near_tap, 6, half - 1).wait_send()
+        bundle(near_conv, conv_buf, 7, groups * half - 1).wait_send()
+
+    @pl.when(upper)
+    def _():
+        bundle(conv_send, conv_buf, 3, groups * half - 1).wait_send()
+
     bundle(spec_send, spec_out, 4, count - 1).wait_send()
     own.wait()
     store.wait()
@@ -546,11 +661,15 @@
             chunk,
             chunk,
             chunk,
+            pltpu.VMEM((count // 2, part, rows), jnp.float32),
+            pltpu.VMEM((shards // 2, part, rows), jnp.float32),
+            pltpu.VMEM((count // 2, part, rows), jnp.float32),
             pltpu.VMEM((residues * height, 2 * rows), jnp.float32),
             pltpu.VMEM((residues * height, 2 * rows), jnp.float32),
             pltpu.VMEM((residues * part, 2 * rows), jnp.float32),
-            pltpu.SemaphoreType.DMA((5,)),
-            pltpu.SemaphoreType.DMA((5,)),
+            pltpu.SemaphoreType.DMA((8,)),
+            pltpu.SemaphoreType.DMA((7,)),
+            pltpu.SemaphoreType.REGULAR,
         ],
         compiler_params=pltpu.CompilerParams(collective_id=0, has_side_effects=True),
     )(*operands)
@@ -579,7 +698,7 @@
     fits = (
         sequences.shape[0] == 1
         and w_out.shape[0] == FULL_TILE * count
-        and lax.axis_size("seq") % 2 == 0
+        and lax.axis_size("seq") % 4 == 0
         and rows % 128 == 0
         and rows % groups == 0
         and 2 * (rows // groups) % 128 == 0

time: 36 us -> 35.1 us (0.975)
  the two profiles are of different devices: /device:TPU:0 before, /device:TPU:25 now
where the time goes in v1:
time: 35.1 us; the launch traced here: 34.9 us
  Pallas kernels  34.2 us (97%)
  between operations  0.64 us (2%)
    pallas_call x1, Pallas kernels, direct(): pl.pallas_call(functools.partial(kernel, groups, shards, part), out_shape...  32.4 us
    pallas_call x1, Pallas kernels, direct(): pl.pallas_call(finish, out_shape=(jax.ShapeDtypeStruct((1, rows, channels...  1.85 us

profile of v1, /device:TPU:25, one launch (start us, length us, event | category | flops | bytes accessed | tf_op | source)
XLA Modules:
  0.0 34.9 jit_solution(14588789303333776431)
XLA Ops:
  0.6 32.4 %shard_map.95 = (bf16[1,256,256]{2,1,0:T(8,128)(2,1)}, f32[32,8,256]{2,1,0:T(8,128)}) custom-call(bf16[1,256,256]{2,1,0:T(8,128)(2,1)} %x_hbm.1, f32[256,256]{1,0:T(8,128)} %taps_hbm.1, bf16[256,768]{1,0:T(8,128)(2,1)} %w_in_hbm.1, bf16[256,256]{1,0:T(8,128)(2,1)} %w_out_hbm.1, bf16[1,256,256]{2,1,0:T(8,128)(2,1)} %cot_hbm.1, ...), custom_call_target="tpu_custom_call" | custom-call | tf_op jit(solution)/shard_map/pallas_call | solution.py:641
  33.0 1.9 %shard_map.96 = (bf16[1,256,256]{2,1,0:T(8,128)(2,1)}, f32[2,2,64,256]{3,2,1,0:T(8,128)}) custom-call(bf16[1,256,256]{2,1,0:T(8,128)(2,1)} %get-tuple-element.4.raw_hbm, f32[32,8,256]{2,1,0:T(8,128)} %get-tuple-element.5.spec_hbm), custom_call_target="tpu_custom_call" | custom-call | tf_op jit(solution)/shard_map/pallas_call | solution.py:676

commit v2 on v1

--- a/solution.py
+++ b/solution.py
@@ -401,8 +401,16 @@
     def _():
         push(sig_send, sig_buf, 0, next_plane)
 
+    @pl.when(upper)
+    def _():
+        push_taps(range(1, shards))
+
     push(cot_send, cot_buf, 2, far)
-    push_taps(range(1, shards))
+
+    @pl.when(lower)
+    def _():
+        push_taps(range(1, shards))
+
     push(cot_send, cot_buf, 2, near)
     cot_buf[me] = cot_send[me]
 
@@ -505,17 +513,17 @@
     by_source = sig_buf[...].reshape(groups, shards, part, rows)
     sig_spec[...] = forward([by_source[:, a] for a in range(shards)], height)
 
-    bundle(tap_send, tap_buf, 1, shards - 1).wait_recv()
-    tap_blocks = tap_buf[...]
-    tap_spec[...] = forward([tap_blocks[a][None] for a in range(shards)], part)
-    convolve(shards, conv_send, shards)
+    def respond():
+        bundle(tap_send, tap_buf, 1, shards - 1).wait_recv()
+        tap_blocks = tap_buf[...]
+        tap_spec[...] = forward([tap_blocks[a][None] for a in range(shards)], part)
+        convolve(shards, conv_send, shards)
 
     @pl.when(lower)
     def _():
-        push(conv_send, conv_buf, 3, far)
-
-    push(conv_send, conv_buf, 3, near)
-    conv_buf[me] = conv_send[me]
+        respond()
+        push(conv_send, conv_buf, 3, far + near)
+        conv_buf[me] = conv_send[me]
 
     factor = 1.0 / (2 * shards * rows)
     residues = shards + 1
@@ -558,6 +566,13 @@
             ]
             spec_send[group * shards + shard] = jnp.concatenate(pieces, axis=1)
     push(spec_send, spec_out, 4, far + near)
+
+    @pl.when(upper)
+    def _():
+        respond()
+        push(conv_send, conv_buf, 3, near)
+        conv_buf[me] = conv_send[me]
+
     own = pltpu.make_async_copy(spec_send.at[me], spec_out.at[me], store_sems.at[0])
     own.start()
 

time: 35.1 us -> 33.8 us (0.963)
  Pallas kernels: 34.2 us -> 33 us
    pallas_call x1, Pallas kernels: 32.4 us -> 31.2 us  [direct(): pl.pallas_call(functools.partial(kernel, groups, shards, part), out_shape...]
where the time goes in v2:
time: 33.8 us; the launch traced here: 33.7 us
  Pallas kernels  33 us (98%)
  between operations  0.64 us (2%)
    pallas_call x1, Pallas kernels, direct(): pl.pallas_call(functools.partial(kernel, groups, shards, part), out_shape...  31.2 us
    pallas_call x1, Pallas kernels, direct(): pl.pallas_call(finish, out_shape=(jax.ShapeDtypeStruct((1, rows, channels...  1.85 us

profile of v2, /device:TPU:25, one launch (start us, length us, event | category | flops | bytes accessed | tf_op | source)
XLA Modules:
  0.0 33.7 jit_solution(17391995514380033320)
XLA Ops:
  0.6 31.2 %shard_map.95 = (bf16[1,256,256]{2,1,0:T(8,128)(2,1)}, f32[32,8,256]{2,1,0:T(8,128)}) custom-call(bf16[1,256,256]{2,1,0:T(8,128)(2,1)} %x_hbm.1, f32[256,256]{1,0:T(8,128)} %taps_hbm.1, bf16[256,768]{1,0:T(8,128)(2,1)} %w_in_hbm.1, bf16[256,256]{1,0:T(8,128)(2,1)} %w_out_hbm.1, bf16[1,256,256]{2,1,0:T(8,128)(2,1)} %cot_hbm.1, ...), custom_call_target="tpu_custom_call" | custom-call | tf_op jit(solution)/shard_map/pallas_call | solution.py:656
  31.8 1.9 %shard_map.96 = (bf16[1,256,256]{2,1,0:T(8,128)(2,1)}, f32[2,2,64,256]{3,2,1,0:T(8,128)}) custom-call(bf16[1,256,256]{2,1,0:T(8,128)(2,1)} %get-tuple-element.4.raw_hbm, f32[32,8,256]{2,1,0:T(8,128)} %get-tuple-element.5.spec_hbm), custom_call_target="tpu_custom_call" | custom-call | tf_op jit(solution)/shard_map/pallas_call | solution.py:691

commit v3 on v2

--- a/solution.py
+++ b/solution.py
@@ -226,9 +226,9 @@
 def kernel(
     groups, shards, part,
     x_hbm, taps_hbm, w_in_hbm, w_out_hbm, cot_hbm, high_hbm, low_hbm, twist_hbm,
-    out_hbm, spec_out,
-    x_ref, taps_ref, w_in_ref, w_out_ref, cot_ref, high_ref, low_ref, twist_ref, out_ref,
-    load_sems, store_sems, query_buf, sig_send, cot_send, tap_send, sig_buf, cot_buf, tap_buf,
+    out_ref, spec_out,
+    x_ref, taps_ref, w_in_ref, w_out_ref, cot_ref, high_ref, low_ref, twist_ref,
+    load_sems, query_buf, sig_send, cot_send, tap_send, sig_buf, cot_buf, tap_buf,
     conv_send, conv_buf, spec_send, near_sig, near_tap, near_conv,
     work, sig_spec, tap_spec, send_sems, recv_sems, late,
 ):
@@ -573,8 +573,7 @@
         push(conv_send, conv_buf, 3, near)
         conv_buf[me] = conv_send[me]
 
-    own = pltpu.make_async_copy(spec_send.at[me], spec_out.at[me], store_sems.at[0])
-    own.start()
+    spec_out[me] = spec_send[me]
 
     @pl.when(lower)
     def _():
@@ -589,8 +588,6 @@
         gated, w_out_ref[...], (((0,), (0,)), ((), ())), preferred_element_type=jnp.float32
     ).astype(jnp.bfloat16)
 
-    store = pltpu.make_async_copy(out_ref, out_hbm, store_sems.at[1])
-    store.start()
     bundle(sig_send, sig_buf, 0, count - 1).wait_send()
     bundle(tap_send, tap_buf, 1, shards - 1).wait_send()
     bundle(cot_send, cot_buf, 2, count - 1).wait_send()
@@ -607,30 +604,19 @@
         bundle(conv_send, conv_buf, 3, groups * half - 1).wait_send()
 
     bundle(spec_send, spec_out, 4, count - 1).wait_send()
-    own.wait()
-    store.wait()
     bundle(spec_send, spec_out, 4, count - 1).wait_recv()
 
 
-def finish(raw_hbm, spec_hbm, out_hbm, grad_hbm, raw_buf, spec_buf, grad_buf, load_sems, store_sems):
-    load_spec = pltpu.make_async_copy(spec_hbm, spec_buf, load_sems.at[0])
-    load_raw = pltpu.make_async_copy(raw_hbm, raw_buf, load_sems.at[1])
-    load_spec.start()
-    load_raw.start()
+def finish(raw_buf, spec_buf, out_hbm, grad_hbm, grad_buf, store_sems):
+    stores = [pltpu.make_async_copy(raw_buf, out_hbm, store_sems.at[2])]
+    stores[0].start()
     count, part, width = spec_buf.shape
-    stores = []
-    load_spec.wait()
     for kind in range(2):
         piece = spec_buf[:, :, kind * (width // 2) : (kind + 1) * (width // 2)]
         grad_buf[kind] = piece.reshape(count * part, width // 2).T.reshape(grad_buf.shape[1:])
         store = pltpu.make_async_copy(grad_buf.at[kind], grad_hbm.at[kind], store_sems.at[kind])
         store.start()
         stores.append(store)
-        if kind == 0:
-            load_raw.wait()
-            store = pltpu.make_async_copy(raw_buf, out_hbm, store_sems.at[2])
-            store.start()
-            stores.append(store)
     for store in stores:
         store.wait()
 
@@ -653,19 +639,18 @@
     chunk = pltpu.VMEM((count, part, rows), jnp.float32)
     height = groups * part
     anywhere = pl.BlockSpec(memory_space=pl.ANY)
+    on_chip = pl.BlockSpec(memory_space=pltpu.VMEM)
     raw, spectra = pl.pallas_call(
         functools.partial(kernel, groups, shards, part),
         out_shape=(
-            jax.ShapeDtypeStruct((1, rows, channels), jnp.bfloat16),
-            jax.ShapeDtypeStruct((count, part, rows), jnp.float32),
+            pltpu.VMEM((1, rows, channels), jnp.bfloat16),
+            pltpu.VMEM((count, part, rows), jnp.float32),
         ),
         in_specs=[anywhere] * 8,
-        out_specs=(anywhere, anywhere),
+        out_specs=(on_chip, on_chip),
         scratch_shapes=[
             *(pltpu.VMEM(item.shape, item.dtype) for item in operands),
-            pltpu.VMEM((1, rows, channels), jnp.bfloat16),
             pltpu.SemaphoreType.DMA((8,)),
-            pltpu.SemaphoreType.DMA((2,)),
             pltpu.VMEM((channels, rows), jnp.float32),
             chunk,
             chunk,
@@ -694,16 +679,16 @@
             jax.ShapeDtypeStruct((1, rows, channels), jnp.bfloat16),
             jax.ShapeDtypeStruct((2, 2, lanes, channels), jnp.float32),
         ),
-        in_specs=[anywhere] * 2,
+        in_specs=[on_chip] * 2,
         out_specs=(anywhere, anywhere),
         scratch_shapes=[
-            pltpu.VMEM(raw.shape, raw.dtype),
-            pltpu.VMEM(spectra.shape, spectra.dtype),
             pltpu.VMEM((2, 2, lanes, channels), jnp.float32),
-            pltpu.SemaphoreType.DMA((2,)),
             pltpu.SemaphoreType.DMA((3,)),
         ],
-    )(raw, spectra)
+    )(
+        pltpu.with_memory_space_constraint(raw, pltpu.VMEM),
+        pltpu.with_memory_space_constraint(spectra, pltpu.VMEM),
+    )
 
 
 def body(sequences, filter_taps, w_in, w_out, grad_out):

time: 33.8 us -> 32.7 us (0.967)
  Pallas kernels: 33 us -> 31.9 us
    pallas_call x1, Pallas kernels: 1.85 us -> 0.83 us  [direct(): pl.pallas_call(finish, out_shape=(jax.ShapeDtypeStruct((1, rows, channels...]
where the time goes in v3:
time: 32.7 us; the launch traced here: 32.5 us
  Pallas kernels  31.9 us (98%)
  between operations  0.64 us (2%)
    pallas_call x1, Pallas kernels, direct(): pl.pallas_call(functools.partial(kernel, groups, shards, part), out_shape...  31.1 us
    pallas_call x1, Pallas kernels, direct(): pl.pallas_call(finish, out_shape=(jax.ShapeDtypeStruct((1, rows, channels...  0.83 us

profile of v3, /device:TPU:25, one launch (start us, length us, event | category | flops | bytes accessed | tf_op | source)
XLA Modules:
  0.0 32.5 jit_solution(11963960340496133639)
XLA Ops:
  0.6 31.1 %shard_map.95 = (bf16[1,256,256]{2,1,0:T(8,128)(2,1)S(1)}, f32[32,8,256]{2,1,0:T(8,128)S(1)}) custom-call(bf16[1,256,256]{2,1,0:T(8,128)(2,1)} %x_hbm.1, f32[256,256]{1,0:T(8,128)} %taps_hbm.1, bf16[256,768]{1,0:T(8,128)(2,1)} %w_in_hbm.1, bf16[256,256]{1,0:T(8,128)(2,1)} %w_out_hbm.1, bf16[1,256,256]{2,1,0:T(8,128)(2,1)} %cot_hbm.1, ...), custom_call_target="tpu_custom_call" | custom-call | tf_op jit(solution)/shard_map/pallas_call | solution.py:643
  31.7 0.8 %shard_map.96 = (bf16[1,256,256]{2,1,0:T(8,128)(2,1)}, f32[2,2,64,256]{3,2,1,0:T(8,128)}) custom-call(bf16[1,256,256]{2,1,0:T(8,128)(2,1)S(1)} %get-tuple-element.4.raw_buf, f32[32,8,256]{2,1,0:T(8,128)S(1)} %get-tuple-element.5.spec_buf), custom_call_target="tpu_custom_call" | custom-call | tf_op jit(solution)/shard_map/pallas_call | solution.py:676

commit v4 on v3

--- a/solution.py
+++ b/solution.py
@@ -230,7 +230,7 @@
     x_ref, taps_ref, w_in_ref, w_out_ref, cot_ref, high_ref, low_ref, twist_ref,
     load_sems, query_buf, sig_send, cot_send, tap_send, sig_buf, cot_buf, tap_buf,
     conv_send, conv_buf, spec_send, near_sig, near_tap, near_conv,
-    work, sig_spec, tap_spec, send_sems, recv_sems, late,
+    work, sig_spec, tap_spec, near_sig_spec, near_tap_spec, send_sems, recv_sems, late,
 ):
     count = groups * shards
     rows = x_ref.shape[1]
@@ -312,9 +312,10 @@
                 device_id_type=MESH,
             ).start()
 
-    def push_taps(offsets):
-        for offset in offsets:
-            shard = lax.rem(my_shard + offset, shards)
+    def push_taps(turns, opposite):
+        base = (my_half + opposite - 2 * my_half * opposite) * half
+        for turn in turns:
+            shard = base + lax.rem(my_shard + turn, half)
             pltpu.make_async_remote_copy(
                 src_ref=tap_send.at[my_group * shards + shard],
                 dst_ref=tap_buf.at[my_shard],
@@ -378,7 +379,9 @@
 
     @pl.when(upper)
     def _():
-        push(sig_send, sig_buf, 0, far + same_plane)
+        push(sig_send, sig_buf, 0, far)
+        push_taps(range(half), 1)
+        push(sig_send, sig_buf, 0, same_plane)
 
     sig_buf[me] = sig_send[me]
     tap_buf[my_shard] = tap_send[me]
@@ -401,17 +404,22 @@
     def _():
         push(sig_send, sig_buf, 0, next_plane)
 
+    @pl.when(lower)
+    def _():
+        push_taps(range(1, half), 0)
+
+    push(cot_send, cot_buf, 2, far)
+
+    @pl.when(lower)
+    def _():
+        push_taps(range(half), 1)
+
+    push(cot_send, cot_buf, 2, near)
+
     @pl.when(upper)
     def _():
-        push_taps(range(1, shards))
-
-    push(cot_send, cot_buf, 2, far)
-
-    @pl.when(lower)
-    def _():
-        push_taps(range(1, shards))
-
-    push(cot_send, cot_buf, 2, near)
+        push_taps(range(1, half), 0)
+
     cot_buf[me] = cot_send[me]
 
     def multiply(value):
@@ -452,16 +460,16 @@
 
     height = groups * part
 
-    def convolve(bands, target, stride):
+    def convolve(bands, sig_from, tap_from, target):
         turns = math.pi / bands
         scale = 1.0 / (2 * bands * rows)
         used = pl.ds(0, (bands + 1) * height)
         for index in range(bands + 1):
             weight = scale if index in (0, bands) else 2.0 * scale
-            tap_part = tap_spec[pl.ds(index * part, part), :] * weight
+            tap_part = tap_from[pl.ds(index * part, part), :] * weight
             real_tap = tap_part[None, :, :rows]
             imag_tap = tap_part[None, :, rows:]
-            sig_part = sig_spec[pl.ds(index * height, height), :].reshape(groups, part, 2 * rows)
+            sig_part = sig_from[pl.ds(index * height, height), :].reshape(groups, part, 2 * rows)
             real_sig = sig_part[:, :, :rows]
             imag_sig = sig_part[:, :, rows:]
             place_at = pl.ds(index * height, height)
@@ -483,21 +491,37 @@
                 + [-math.sin(turns * (a * i % (2 * bands))) for i in range(bands + 1)],
             )
             for group in range(groups):
-                target[group * stride + a] = value[group]
+                target[group * bands + a] = value[group]
+
+    bundle(sig_send, sig_buf, 0, count - 1).wait_recv()
+    by_source = sig_buf[...].reshape(groups, shards, part, rows)
+    sig_spec[...] = forward([by_source[:, a] for a in range(shards)], height)
+
+    def respond():
+        bundle(tap_send, tap_buf, 1, shards - 1).wait_recv()
+        tap_blocks = tap_buf[...]
+        tap_spec[...] = forward([tap_blocks[a][None] for a in range(shards)], part)
+        convolve(shards, sig_spec, tap_spec, conv_send)
+
+    @pl.when(lower)
+    def _():
+        respond()
+        push(conv_send, conv_buf, 3, far + near)
+        conv_buf[me] = conv_send[me]
 
     @pl.when(lower)
     def _():
         bundle(sig_send, near_sig, 5, groups * half - 1).wait_recv()
         by_source = near_sig[...].reshape(groups, half, part, rows)
-        sig_spec[pl.ds(0, (half + 1) * height), :] = forward(
+        near_sig_spec[...] = forward(
             [by_source[:, a] for a in range(half)], height
         )
         bundle(tap_send, near_tap, 6, half - 1).wait_recv()
         tap_blocks = near_tap[...]
-        tap_spec[pl.ds(0, (half + 1) * part), :] = forward(
+        near_tap_spec[...] = forward(
             [tap_blocks[a][None] for a in range(half)], part
         )
-        convolve(half, near_conv, half)
+        convolve(half, near_sig_spec, near_tap_spec, near_conv)
         for group, shard in near:
             pltpu.make_async_remote_copy(
                 src_ref=near_conv.at[group * half + shard],
@@ -508,22 +532,6 @@
                 device_id_type=MESH,
             ).start()
         conv_buf[me + half] = near_conv[near_me]
-
-    bundle(sig_send, sig_buf, 0, count - 1).wait_recv()
-    by_source = sig_buf[...].reshape(groups, shards, part, rows)
-    sig_spec[...] = forward([by_source[:, a] for a in range(shards)], height)
-
-    def respond():
-        bundle(tap_send, tap_buf, 1, shards - 1).wait_recv()
-        tap_blocks = tap_buf[...]
-        tap_spec[...] = forward([tap_blocks[a][None] for a in range(shards)], part)
-        convolve(shards, conv_send, shards)
-
-    @pl.when(lower)
-    def _():
-        respond()
-        push(conv_send, conv_buf, 3, far + near)
-        conv_buf[me] = conv_send[me]
 
     factor = 1.0 / (2 * shards * rows)
     residues = shards + 1
@@ -667,6 +675,8 @@
             pltpu.VMEM((residues * height, 2 * rows), jnp.float32),
             pltpu.VMEM((residues * height, 2 * rows), jnp.float32),
             pltpu.VMEM((residues * part, 2 * rows), jnp.float32),
+            pltpu.VMEM(((shards // 2 + 1) * height, 2 * rows), jnp.float32),
+            pltpu.VMEM(((shards // 2 + 1) * part, 2 * rows), jnp.float32),
             pltpu.SemaphoreType.DMA((8,)),
             pltpu.SemaphoreType.DMA((7,)),
             pltpu.SemaphoreType.REGULAR,

time: 32.7 us -> 31.6 us (0.966)
  Pallas kernels: 31.9 us -> 30.9 us
    pallas_call x1, Pallas kernels: 31.1 us -> 30 us  [direct(): pl.pallas_call(functools.partial(kernel, groups, shards, part), out_shape...]
where the time goes in v4:
time: 31.6 us; the launch traced here: 31.5 us
  Pallas kernels  30.9 us (98%)
  between operations  0.64 us (2%)
    pallas_call x1, Pallas kernels, direct(): pl.pallas_call(functools.partial(kernel, groups, shards, part), out_shape...  30 us
    pallas_call x1, Pallas kernels, direct(): pl.pallas_call(finish, out_shape=(jax.ShapeDtypeStruct((1, rows, channels...  0.83 us

profile of v4, /device:TPU:25, one launch (start us, length us, event | category | flops | bytes accessed | tf_op | source)
XLA Modules:
  0.0 31.5 jit_solution(4224653339474546697)
XLA Ops:
  0.6 30.0 %shard_map.95 = (bf16[1,256,256]{2,1,0:T(8,128)(2,1)S(1)}, f32[32,8,256]{2,1,0:T(8,128)S(1)}) custom-call(bf16[1,256,256]{2,1,0:T(8,128)(2,1)} %x_hbm.1, f32[256,256]{1,0:T(8,128)} %taps_hbm.1, bf16[256,768]{1,0:T(8,128)(2,1)} %w_in_hbm.1, bf16[256,256]{1,0:T(8,128)(2,1)} %w_out_hbm.1, bf16[1,256,256]{2,1,0:T(8,128)(2,1)} %cot_hbm.1, ...), custom_call_target="tpu_custom_call" | custom-call | tf_op jit(solution)/shard_map/pallas_call | solution.py:651
  30.7 0.8 %shard_map.96 = (bf16[1,256,256]{2,1,0:T(8,128)(2,1)}, f32[2,2,64,256]{3,2,1,0:T(8,128)}) custom-call(bf16[1,256,256]{2,1,0:T(8,128)(2,1)S(1)} %get-tuple-element.4.raw_buf, f32[32,8,256]{2,1,0:T(8,128)S(1)} %get-tuple-element.5.spec_buf), custom_call_target="tpu_custom_call" | custom-call | tf_op jit(solution)/shard_map/pallas_call | solution.py:686

commit v5 on v4

--- a/solution.py
+++ b/solution.py
@@ -573,7 +573,19 @@
                 for index in (2 * shard, 2 * shard + 1)
             ]
             spec_send[group * shards + shard] = jnp.concatenate(pieces, axis=1)
-    push(spec_send, spec_out, 4, far + near)
+
+    def line(turn):
+        shard = ((1 - my_half) * 2 + turn // quarter) * quarter + turn % quarter
+        return [(lax.rem(my_group + c, groups), shard) for c in range(groups)]
+
+    @pl.when(lower)
+    def _():
+        turns = [quarter, *range(quarter), *range(quarter + 1, 2 * quarter)]
+        push(spec_send, spec_out, 4, [peer for turn in turns for peer in line(turn)] + near)
+
+    @pl.when(upper)
+    def _():
+        push(spec_send, spec_out, 4, far + near)
 
     @pl.when(upper)
     def _():

time: 31.6 us -> 31.4 us (level)
  the two profiles are of different devices: /device:TPU:25 before, /device:TPU:0 now
where the time goes in v5:
time: 31.4 us; the launch traced here: 31.2 us
  Pallas kernels  30.6 us (97%)
  between operations  0.64 us (2%)
    pallas_call x1, Pallas kernels, direct(): pl.pallas_call(functools.partial(kernel, groups, shards, part), out_shape...  29.7 us
    pallas_call x1, Pallas kernels, direct(): pl.pallas_call(finish, out_shape=(jax.ShapeDtypeStruct((1, rows, channels...  0.83 us

profile of v5, /device:TPU:0, one launch (start us, length us, event | category | flops | bytes accessed | tf_op | source)
XLA Modules:
  0.0 31.2 jit_solution(5824611006098875827)
XLA Ops:
  0.6 29.7 %shard_map.95 = (bf16[1,256,256]{2,1,0:T(8,128)(2,1)S(1)}, f32[32,8,256]{2,1,0:T(8,128)S(1)}) custom-call(bf16[1,256,256]{2,1,0:T(8,128)(2,1)} %x_hbm.1, f32[256,256]{1,0:T(8,128)} %taps_hbm.1, bf16[256,768]{1,0:T(8,128)(2,1)} %w_in_hbm.1, bf16[256,256]{1,0:T(8,128)(2,1)} %w_out_hbm.1, bf16[1,256,256]{2,1,0:T(8,128)(2,1)} %cot_hbm.1, ...), custom_call_target="tpu_custom_call" | custom-call | tf_op jit(solution)/shard_map/pallas_call | solution.py:663
  30.4 0.8 %shard_map.96 = (bf16[1,256,256]{2,1,0:T(8,128)(2,1)}, f32[2,2,64,256]{3,2,1,0:T(8,128)}) custom-call(bf16[1,256,256]{2,1,0:T(8,128)(2,1)S(1)} %get-tuple-element.4.raw_buf, f32[32,8,256]{2,1,0:T(8,128)S(1)} %get-tuple-element.5.spec_buf), custom_call_target="tpu_custom_call" | custom-call | tf_op jit(solution)/shard_map/pallas_call | solution.py:698
